TPU v7x, 32 devices: a whole 2x2x4 slice. The times are simulated.
32 devices in a mesh: groups: 2 (over y), seq: 4 (over z), head: 2 (over x), dp: 2 (over core).
Axes of the slice: x: 2, y: 2, z: 4, core: 2. Of those that a mesh axis runs over, the one named last changes fastest.
Arguments:
- queries: bfloat16 [4, 2048, 512], P(('groups', 'dp'), 'seq', 'head'), parts along dimension 0, may hold values from -6 to 6
- key_rows: bfloat16 [4, 2048, 512], P(('groups', 'dp'), 'seq', 'head'), parts along dimension 0, may hold values from -6 to 6
- value_rows: bfloat16 [4, 2048, 512], P(('groups', 'dp'), 'seq', 'head'), parts along dimension 0, may hold values from -6 to 6
- layout: int32 [4, 8, 4], P('head'), may hold values from 0 to 7
- out_weight: bfloat16 [4096, 512], P(None, 'head'), may hold values from -0.25 to 0.25
- out_grad: bfloat16 [4, 2048, 4096], P(('groups', 'dp'), 'seq', 'head'), parts along dimension 0, may hold values from -6 to 6
Outputs:
- attn: bfloat16 [4, 2048, 512], P(('groups', 'dp'), 'seq', 'head'), parts along dimension 0
- query_grad: bfloat16 [4, 2048, 512], P(('groups', 'dp'), 'seq', 'head'), parts along dimension 0
- key_grad: bfloat16 [4, 2048, 512], P(('groups', 'dp'), 'seq', 'head'), parts along dimension 0
- value_grad: bfloat16 [4, 2048, 512], P(('groups', 'dp'), 'seq', 'head'), parts along dimension 0
- weight_grad: float32 [8192, 512], P(('groups', 'seq', 'dp'), 'head'), parts along dimension 0
There are 2 independent parts, one for each index of `groups`. A program takes and returns all parts, laid end to end along the dimension named above; an argument that names none is the same for every part. Nothing has to cross between parts.
Inputs may be any that keep to these rules, and one draw needn't show every extreme that they name: layout[h, i, j] names a key-value block of the same sequence that query block i of head h reads; entries may repeat and may name any block.
All inputs are finite; a program needn't handle non-finite values.
Results may differ from a plain program's by a relative error of at most 0.018.
Values may be sent and summed in bfloat16 or wider, within the bound.
No kernel may reach another device: no remote copies, remote signals or barrier semaphores. Data moves between devices by JAX's collectives and lax.ppermute only.
A program may use at most 64 MiB of HBM per device.

v0:
```python
import jax
import jax.numpy as jnp
from jax import lax
from jax.sharding import PartitionSpec as P

DH = 128
BLK = 256
epsilon = 1e-06


def feature_map(inputs):
    return jnp.where(inputs > 0, inputs + 1.0, jnp.exp(jnp.minimum(inputs, 0.0)))


def feature_slope(inputs):
    return jnp.where(inputs > 0, 1.0, jnp.exp(jnp.minimum(inputs, 0.0)))


def per_device(queries, key_rows, value_rows, layout, out_weight, out_grad):
    highest = lax.Precision.HIGHEST
    f32 = jnp.float32
    bf16 = jnp.bfloat16
    seq_count = lax.axis_size("seq")
    seq_index = lax.axis_index("seq")
    heads_here = layout.shape[0]
    block_total = layout.shape[1]
    tokens_here = queries.shape[1]
    block_count = tokens_here // BLK
    my_first = seq_index * block_count
    counts = jnp.sum(
        (layout[..., None] == jnp.arange(block_total, dtype=jnp.int32)).astype(f32), axis=2
    )
    owner_cols = lax.dynamic_slice_in_dim(counts, my_first, block_count, 2)
    causal = jnp.tril(jnp.ones((BLK, BLK), f32))
    query_in = queries[0].astype(f32).reshape(block_count, BLK, heads_here, DH)
    key_in = key_rows[0].astype(f32).reshape(block_count, BLK, heads_here, DH)
    value_b = value_rows[0].reshape(block_count, BLK, heads_here, DH)
    query_feat = feature_map(query_in).astype(bf16)
    key_feat = feature_map(key_in).astype(bf16)
    states = jnp.einsum("nthd,nthe->nhde", key_feat, value_b, preferred_element_type=f32)
    presum = jnp.einsum("hqm,mhde->qhde", owner_cols, states, precision=highest)
    presum = presum.reshape(seq_count, block_count, heads_here, DH, DH)
    arrived = lax.all_to_all(presum, "seq", split_axis=0, concat_axis=0, tiled=True)
    carried = jnp.sum(arrived, axis=0)
    carried_b = carried.astype(bf16)
    scores = (
        jnp.einsum("nthd,nshd->nhts", query_feat, key_feat, preferred_element_type=f32) * causal
    )
    scores_b = scores.astype(bf16)
    numer = jnp.einsum("nthd,nhde->nthe", query_feat, carried_b, preferred_element_type=f32)
    numer = numer + jnp.einsum("nhts,nshe->nthe", scores_b, value_b, preferred_element_type=f32)
    rinv = lax.rsqrt(jnp.mean(numer * numer, axis=-1, keepdims=True) + epsilon)
    attn_out = (numer * rinv).astype(bf16)
    attn_flat = attn_out.reshape(tokens_here, heads_here * DH)
    gathered = lax.all_gather(out_grad, "head", axis=2, tiled=True)
    grad_rows = gathered[0]
    d_attn = jnp.dot(grad_rows, out_weight, preferred_element_type=f32).astype(bf16)
    grad_f = d_attn.astype(f32).reshape(block_count, BLK, heads_here, DH)
    d_numer = rinv * grad_f - numer * rinv**3 * jnp.mean(grad_f * numer, axis=-1, keepdims=True)
    d_numer = d_numer.astype(bf16)
    c_grad = jnp.einsum("nthd,nthe->nhde", query_feat, d_numer, preferred_element_type=f32)
    s_grad = jnp.einsum(
        "hmk,mhde->khde",
        owner_cols,
        lax.all_gather(c_grad, "seq", axis=0, tiled=True),
        precision=highest,
    )
    s_grad_b = s_grad.astype(bf16)
    p_grad = (
        jnp.einsum("nthe,nshe->nhts", d_numer, value_b, preferred_element_type=f32) * causal
    ).astype(bf16)
    dq_feat = jnp.einsum("nthe,nhde->nthd", d_numer, carried_b, preferred_element_type=f32)
    dq_feat = dq_feat + jnp.einsum("nhts,nshd->nthd", p_grad, key_feat, preferred_element_type=f32)
    dk_feat = jnp.einsum("nshe,nhde->nshd", value_b, s_grad_b, preferred_element_type=f32)
    dk_feat = dk_feat + jnp.einsum(
        "nhts,nthd->nshd", p_grad, query_feat, preferred_element_type=f32
    )
    dv_full = jnp.einsum("nshd,nhde->nshe", key_feat, s_grad_b, preferred_element_type=f32)
    dv_full = dv_full + jnp.einsum("nhts,nthe->nshe", scores_b, d_numer, preferred_element_type=f32)
    flat_shape = (1, tokens_here, heads_here * DH)
    query_grad = (dq_feat * feature_slope(query_in)).astype(bf16).reshape(flat_shape)
    key_grad = (dk_feat * feature_slope(key_in)).astype(bf16).reshape(flat_shape)
    value_grad = dv_full.astype(bf16).reshape(flat_shape)
    weight_grad = lax.psum_scatter(
        lax.dot_general(
            grad_rows, attn_flat, (((0,), (0,)), ((), ())), preferred_element_type=f32
        ).astype(jnp.bfloat16),
        ("seq", "dp"),
        scatter_dimension=0,
        tiled=True,
    ).astype(jnp.float32)
    return (attn_flat.reshape(flat_shape), query_grad, key_grad, value_grad, weight_grad)


def solution(mesh):
    placed = (
        P(("groups", "dp"), "seq", "head"),
        P(("groups", "dp"), "seq", "head"),
        P(("groups", "dp"), "seq", "head"),
        P("head", None, None),
        P(None, "head"),
        P(("groups", "dp"), "seq", "head"),
    )
    return jax.shard_map(
        per_device,
        mesh=mesh,
        in_specs=placed,
        out_specs=(
            P(("groups", "dp"), "seq", "head"),
            P(("groups", "dp"), "seq", "head"),
            P(("groups", "dp"), "seq", "head"),
            P(("groups", "dp"), "seq", "head"),
            P(("groups", "seq", "dp"), "head"),
        ),
        check_vma=False,
    )
```

profile of v0, /device:TPU:0, one launch (start us, length us, event | category | flops | bytes accessed | tf_op | source)
XLA Modules:
  0.0 156.0 jit_solution(2445478102337339927)
XLA Ops:
  7.9 1.9 %fusion.26 = (f32[1,512,256]{2,1,0:T(8,128)}, bf16[1,512,256]{2,1,0:T(8,128)(2,1)S(1)}) fusion(bf16[1,512,256]{2,1,0:T(8,128)(2,1)} %param.7), kind=kLoop, calls=%fused_computation.37 | loop fusion | flops 917504 | bytes 1048576 | tf_op jit(solution)/shard_map/jit(_where)/select_n | solution.py:16
  13.0 6.3 %all-to-all-start = ((f32[4,2,2,128,128]{4,1,3,2,0:T(2,128)}), f32[4,2,2,128,128]{4,1,3,2,0:T(2,128)}, u32[]{:S(2)}, u32[]{:S(2)}) async-start(f32[4,2,2,128,128]{4,1,3,2,0:T(2,128)} %copy.90), calls=%async_computation | async-start | bytes 2097152 | tf_op jit(solution)/shard_map/all_to_all | solution.py:43
  19.3 2.0 %fusion.30 = (f32[1,512,256]{2,1,0:T(8,128)}, bf16[1,512,256]{2,1,0:T(8,128)(2,1)S(1)}) fusion(bf16[1,512,256]{2,1,0:T(8,128)(2,1)} %param.6), kind=kLoop, calls=%fused_computation.41 | loop fusion | flops 917504 | bytes 1048576 | tf_op jit(solution)/shard_map/jit(_where)/select_n | solution.py:16
  23.4 21.7 %all-to-all-done = f32[4,2,2,128,128]{4,1,3,2,0:T(2,128)} async-done(((f32[4,2,2,128,128]{4,1,3,2,0:T(2,128)}), f32[4,2,2,128,128]{4,1,3,2,0:T(2,128)}, u32[]{:S(2)}, u32[]{:S(2)}) %all-to-all-start) | async-done | bytes 1048608 | tf_op jit(solution)/shard_map/all_to_all | solution.py:43
  46.8 22.2 %all-gather.3.cloned.1.call-done = bf16[1,512,4096]{2,1,0:T(8,128)(2,1)} async-done(((bf16[1,512,2048]{2,1,0:T(8,128)(2,1)}), bf16[1,512,4096]{2,1,0:T(8,128)(2,1)}) %all-gather.3.cloned.1.call-update) | async-done | bytes 4194320 | tf_op jit(solution)/shard_map/all_gather | solution.py:55
  69.1 4.2 %fusion.16 = f32[512,256]{1,0:T(8,128)} fusion(bf16[4096,256]{1,0:T(8,128)(2,1)S(1)} %copy-done, bf16[1,512,4096]{2,1,0:T(8,128)(2,1)} %all-gather.3.cloned.1.call-done), kind=kOutput, calls=%fused_computation.22 | convolution fusion | flops 1074003968 | bytes 6815744 | tf_op jit(solution)/shard_map/dot_general | solution.py:57
  73.3 2.1 %reshape.94 = f32[2,256,2,128]{3,2,1,0:T(2,128)} reshape(f32[512,256]{1,0:T(8,128)} %fusion.16) | data formatting | bytes 1048576 | tf_op jit(solution)/shard_map/reshape | solution.py:58
  75.4 2.0 %copy.98 = f32[2,256,2,128]{1,3,2,0:T(8,128)} copy(f32[2,256,2,128]{3,2,1,0:T(2,128)} %reshape.94) | data formatting | bytes 1048576 | tf_op jit(solution)/shard_map/reshape | solution.py:58
  79.0 1.9 %subtract_convert_fusion = (bf16[2,256,2,128]{1,3,2,0:T(8,128)(2,1)S(1)}, bf16[2,256,2,128]{1,3,2,0:T(8,128)(2,1)}) fusion(f32[2,256,2,128]{1,3,2,0:T(8,128)S(1)} %get-tuple-element.35, f32[2,256,2,128]{1,3,2,0:T(8,128)} %copy.98, f32[2,256,2]{1,2,0:T(2,128)S(1)} %get-tuple-element.36, f32[2,256,2]{1,2,0:T(2,128)S(1)} %get-tuple-element.33, ...), kind=kLoop, calls=%fused_computation.42 | loop fusion | flops 917504 | bytes 1585152 | tf_op jit(solution)/shard_map/convert_element_type | solution.py:60
  82.1 1.8 %copy.97 = bf16[2,256,2,128]{3,2,1,0:T(2,128)(2,1)} copy(bf16[2,256,2,128]{1,3,2,0:T(8,128)(2,1)} %get-tuple-element.28) | data formatting | bytes 524288 | tf_op jit(solution)/shard_map/convert_element_type | solution.py:53
  83.9 4.9 %fusion = bf16[4096,256]{0,1:T(8,128)(2,1)} fusion(bf16[1,512,4096]{2,1,0:T(8,128)(2,1)} %all-gather.3.cloned.1.call-done, bf16[64,8,2,128]{3,2,1,0:T(2,128)(2,1)} %bitcast.68), kind=kOutput, calls=%fused_computation.1 | convolution fusion | flops 1074790400 | bytes 6553600 | tf_op jit(solution)/shard_map/dot_general | solution.py:85
  88.8 2.1 %select_n.48 = f32[2,256,2,128]{3,2,1,0:T(2,128)} reshape(f32[1,512,256]{2,1,0:T(8,128)} %get-tuple-element.29) | data formatting | bytes 1048576 | tf_op jit(solution)/shard_map/jit(_where)/select_n | solution.py:16
  90.9 2.0 %copy.113 = f32[2,256,2,128]{1,3,2,0:T(8,128)} copy(f32[2,256,2,128]{3,2,1,0:T(2,128)} %select_n.48) | data formatting | bytes 1048576 | tf_op jit(solution)/shard_map/jit(_where)/select_n | solution.py:16
  92.9 2.1 %select_n.46 = f32[2,256,2,128]{3,2,1,0:T(2,128)} reshape(f32[1,512,256]{2,1,0:T(8,128)} %get-tuple-element.31) | data formatting | bytes 1048576 | tf_op jit(solution)/shard_map/jit(_where)/select_n | solution.py:16
  95.0 2.0 %copy.105 = f32[2,256,2,128]{1,3,2,0:T(8,128)} copy(f32[2,256,2,128]{3,2,1,0:T(2,128)} %select_n.46) | data formatting | bytes 1048576 | tf_op jit(solution)/shard_map/jit(_where)/select_n | solution.py:16
  97.1 1.8 %reshape_reshape.3 = bf16[1,512,256]{2,1,0:T(8,128)(2,1)} reshape(bf16[2,256,2,128]{3,2,1,0:T(2,128)(2,1)} %copy.97) | data formatting | bytes 524288 | tf_op jit(solution)/shard_map/reshape;reshape | solution.py:92
  102.2 2.0 %fusion.11 = bf16[2,256,2,128]{1,3,2,0:T(8,128)(2,1)} fusion(f32[2,256,2,128]{1,3,2,0:T(8,128)} %copy.105, f32[2,2,128,256]{3,2,1,0:T(8,128)S(1)} %fusion.51, bf16[2,256,2,128]{1,3,2,0:T(8,128)(2,1)S(1)} %get-tuple-element.27, bf16[2,2,128,128]{3,0,2,1:T(2,128)(2,1)S(1)} %reduce_sum.37), kind=kOutput, calls=%fused_computation.19 | convolution fusion | flops 33947648 | bytes 1703936 | tf_op jit(solution)/shard_map/nthe,nhde->nthd/dot_general | solution.py:72
  104.2 1.8 %copy.106 = bf16[2,256,2,128]{3,2,1,0:T(2,128)(2,1)} copy(bf16[2,256,2,128]{1,3,2,0:T(8,128)(2,1)} %fusion.11) | data formatting | bytes 524288 | tf_op jit(solution)/shard_map/convert_element_type | solution.py:81
  106.0 1.8 %reshape.89 = bf16[1,512,256]{2,1,0:T(8,128)(2,1)} reshape(bf16[2,256,2,128]{3,2,1,0:T(2,128)(2,1)} %copy.106) | data formatting | bytes 524288 | tf_op jit(solution)/shard_map/reshape | solution.py:81
  108.9 2.1 %fusion.53 = f32[2,2,128,256]{3,2,1,0:T(8,128)} fusion(bf16[2,256,2,128]{1,3,2,0:T(8,128)(2,1)S(1)} %copy.107, bf16[2,2,256,256]{3,2,1,0:T(8,128)(2,1)} %copy-done.1), kind=kOutput, calls=%fused_computation.74 | convolution fusion | flops 67108864 | bytes 1310720 | tf_op jit(solution)/shard_map/nhts,nthd->nshd/dot_general | solution.py:75
  111.0 2.9 %fusion.21 = bf16[2,2,128,128]{3,0,2,1:T(2,128)(2,1)S(1)} fusion(f32[8,2,128,128]{3,2,1,0:T(8,128)} %all-gather.5.cloned.1.call-done, f32[2,8,8]{2,1,0:T(8,128)S(1)} %convert_reduce_fusion, s32[]{:T(128)S(6)} %select_n.41), kind=kOutput, calls=%fused_computation.26 | convolution fusion | flops 6356992 | bytes 1180164 | tf_op jit(solution)/shard_map/hmk,mhde->khde/dot_general | solution.py:62
  114.0 2.1 %fusion.20 = bf16[2,256,2,128]{1,3,2,0:T(8,128)(2,1)} fusion(f32[2,2,128,256]{3,2,1,0:T(8,128)} %fusion.54, bf16[2,2,128,128]{2,3,1,0:T(8,128)(2,1)S(1)} %copy.115, bf16[2,256,2,128]{3,2,1,0:T(2,128)(2,1)} %copy-done.2), kind=kOutput, calls=%fused_computation.24 | convolution fusion | flops 33816576 | bytes 1179648 | tf_op jit(solution)/shard_map/nshd,nhde->nshe/dot_general | solution.py:78
  120.4 27.1 %reduce-scatter.2.cloned.1.call-done = bf16[512,256]{0,1:T(8,128)(2,1)} async-done(((bf16[4096,256]{0,1:T(8,128)(2,1)}), bf16[512,256]{0,1:T(8,128)(2,1)}) %reduce-scatter.2.cloned.1.call-update) | async-done | bytes 262160 | tf_op jit(solution)/shard_map/reduce_scatter | solution.py:84
  147.6 1.9 %copy.119 = f32[512,256]{1,0:T(8,128)} copy(bf16[512,256]{0,1:T(8,128)(2,1)} %reduce-scatter.2.cloned.1.call-done) | data formatting | bytes 786432
  (48 shorter events, 19.2 us)
Async XLA Ops:
  7.2 61.9 %copy-start = (bf16[4096,256]{1,0:T(8,128)(2,1)S(1)}, bf16[4096,256]{1,0:T(8,128)(2,1)}, u32[]{:S(2)}) copy-start(bf16[4096,256]{1,0:T(8,128)(2,1)} %param.10) | copy-start | bytes 6291460
  7.2 2.9 %copy-start.6 = (bf16[1,512,256]{2,1,0:T(8,128)(2,1)S(1)}, bf16[1,512,256]{2,1,0:T(8,128)(2,1)}, u32[]{:S(2)}) copy-start(bf16[1,512,256]{2,1,0:T(8,128)(2,1)} %param.8) | copy-start | bytes 786436
  7.2 3.0 %copy-start.7 = (s32[2,8,4]{1,2,0:T(4,128)S(1)}, s32[2,8,4]{1,2,0:T(4,128)}, u32[]{:S(2)}) copy-start(s32[2,8,4]{1,2,0:T(4,128)} %param.9) | copy-start | bytes 772
  7.2 61.9 %all-gather.3.cloned.1.call-start = ((), (), s32[]{:S(2)}) async-start(), calls=%async_computation.2 | async-start | bytes 6291456 | tf_op jit(solution)/shard_map/all_gather | solution.py:55
  9.9 11.6 %copy-start.2 = (bf16[2,256,2,128]{3,2,1,0:T(2,128)(2,1)}, bf16[2,256,2,128]{3,2,1,0:T(2,128)(2,1)S(1)}, u32[]{:S(2)}) copy-start(bf16[2,256,2,128]{3,2,1,0:T(2,128)(2,1)S(1)} %select_n.40) | copy-start | bytes 786436
  10.1 11.2 %copy-start.3 = (bf16[2,256,2,128]{1,3,2,0:T(8,128)(2,1)}, bf16[2,256,2,128]{1,3,2,0:T(8,128)(2,1)S(1)}, u32[]{:S(2)}) copy-start(bf16[2,256,2,128]{1,3,2,0:T(8,128)(2,1)S(1)} %copy.86) | copy-start | bytes 786436
  13.0 32.1 %all-to-all-start = ((f32[4,2,2,128,128]{4,1,3,2,0:T(2,128)}), f32[4,2,2,128,128]{4,1,3,2,0:T(2,128)}, u32[]{:S(2)}, u32[]{:S(2)}) async-start(f32[4,2,2,128,128]{4,1,3,2,0:T(2,128)} %copy.90), calls=%async_computation | async-start | bytes 2097152 | tf_op jit(solution)/shard_map/all_to_all | solution.py:43
  19.3 91.7 %all-gather.5.cloned.1.call-start = ((), (), s32[]{:S(2)}) async-start(), calls=%async_computation.3 | async-start | bytes 1310720 | tf_op jit(solution)/shard_map/all_gather | solution.py:65
  21.5 0.7 copy-start.4
  81.8 65.8 %reduce-scatter.2.cloned.1.call-start = ((), (), s32[]{:S(2)}) async-start(), calls=%async_computation.4 | async-start | bytes 2359296 | tf_op jit(solution)/shard_map/reduce_scatter | solution.py:84
  100.2 0.8 copy-start.1
  108.9 9.2 %copy-start.5 = (f32[2,256,2,128]{1,3,2,0:T(8,128)S(1)}, f32[2,256,2,128]{1,3,2,0:T(8,128)}, u32[]{:S(2)}) copy-start(f32[2,256,2,128]{1,3,2,0:T(8,128)} %copy.113) | copy-start | bytes 1572868
Sparse Core Ops, SparseCore 0:
  9.6 59.4 all-gather.2
  81.9 27.9 all-gather.4
  112.2 35.3 reduce-scatter.1
where the time goes:
time: 157 us; the launch traced here: 156 us
  waiting for transfers between devices  71.8 us (46%)
  matrix products  28.3 us (18%)
  local copies, waits for them, and re-layouts  27.8 us (18%)
  between operations  14 us (9%)
  other arithmetic  7.58 us (5%)
  starting transfers between devices  6.58 us (4%)
    reduce_scatter x1, waiting for transfers between devices, per_device(): lax.psum_scatter(lax.dot_general(grad_rows, attn_flat, (((0,), (0,)), (()...  27.1 us
    all_gather x1, waiting for transfers between devices, per_device(): gathered = lax.all_gather(out_grad, 'head', axis=2, tiled=True)  22.2 us
    all_to_all x1, waiting for transfers between devices, per_device(): lax.all_to_all(presum, 'seq', split_axis=0, concat_axis=0, tiled=True)  21.7 us
    select_n x4, local copies, waits for them, and re-layouts, feature_slope(): return jnp.where(inputs > 0, 1.0, jnp.exp(jnp.minimum(inputs, 0.0)))  8.28 us
    all_to_all x1, starting transfers between devices, per_device(): lax.all_to_all(presum, 'seq', split_axis=0, concat_axis=0, tiled=True)  6.32 us
    dot_general x1, matrix products, per_device(): lax.dot_general(grad_rows, attn_flat, (((0,), (0,)), ((), ())), preferred...  4.88 us
    dot_general x1, matrix products, per_device(): jnp.dot(grad_rows, out_weight, preferred_element_type=f32).astype(bf16)  4.23 us
    reshape x2, local copies, waits for them, and re-layouts, per_device(): grad_f = d_attn.astype(f32).reshape(block_count, BLK, heads_here, DH)  4.13 us
  transfers between devices with their start and end apart: 4, of which 3 were waited for; matrix products, arithmetic and copies ran while one was open for 31% of the time, Pallas kernels for 0%

commit v1 on v0

--- a/solution.py
+++ b/solution.py
@@ -6,6 +6,24 @@
 DH = 128
 BLK = 256
 epsilon = 1e-06
+
+
+def laid_out(pieces, dim):
+    dims = list(pieces.shape[1:])
+    dims[dim] *= pieces.shape[0]
+    return jnp.moveaxis(pieces, 0, dim).reshape(dims)
+
+
+def grow_blocks(array, axis):
+    size = lax.axis_size(axis)
+    blocks = array[None]
+    for level in range(size.bit_length() - 1):
+        bit = 1 << level
+        other = lax.ppermute(blocks, axis, [(i, i ^ bit) for i in range(size)])
+        both = jnp.stack([blocks, other])
+        upper = lax.axis_index(axis) >> level & 1
+        blocks = jnp.where(upper == 0, both, both[::-1]).reshape(-1, *array.shape)
+    return blocks
 
 
 def feature_map(inputs):
@@ -52,7 +70,7 @@
     rinv = lax.rsqrt(jnp.mean(numer * numer, axis=-1, keepdims=True) + epsilon)
     attn_out = (numer * rinv).astype(bf16)
     attn_flat = attn_out.reshape(tokens_here, heads_here * DH)
-    gathered = lax.all_gather(out_grad, "head", axis=2, tiled=True)
+    gathered = laid_out(grow_blocks(out_grad, "head"), 2)
     grad_rows = gathered[0]
     d_attn = jnp.dot(grad_rows, out_weight, preferred_element_type=f32).astype(bf16)
     grad_f = d_attn.astype(f32).reshape(block_count, BLK, heads_here, DH)

time: 157 us -> 141 us (0.90)
  waiting for transfers between devices: 71.8 us -> 50.6 us
  matrix products: 28.3 us -> 24.3 us
  other arithmetic: 7.58 us -> 10.8 us
  local copies, waits for them, and re-layouts: 27.8 us -> 31 us
  between operations: 14 us -> 15.7 us
    all_gather x1 -> x0, waiting for transfers between devices: 22.2 us -> none  [per_device(): gathered = lax.all_gather(out_grad, 'head', axis=2, tiled=True)]
    reduce_scatter x1, waiting for transfers between devices: 27.1 us -> 11.5 us  [per_device(): lax.psum_scatter(lax.dot_general(grad_rows, attn_flat, (((0,), (0,)), (()...]
    ppermute x0 -> x1, waiting for transfers between devices: none -> 9.71 us  [grow_blocks(): other = lax.ppermute(blocks, axis, [(i, i ^ bit) for i in range(size)])]
    all_gather x1, waiting for transfers between devices: 0.01 us -> 6.96 us  [per_device(): lax.all_gather(c_grad, 'seq', axis=0, tiled=True)]
    unnamed x17 -> x25, local copies, waits for them, and re-layouts: 3.06 us -> 7.22 us
    ppermute x0 -> x1, starting transfers between devices: none -> 2.94 us  [grow_blocks(): other = lax.ppermute(blocks, axis, [(i, i ^ bit) for i in range(size)])]
    another operation x0 -> x1, other arithmetic: none -> 2.61 us  [grow_blocks(): both = jnp.stack([blocks, other])]
    dot_general x1, matrix products: 4.23 us -> 2.08 us  [per_device(): jnp.dot(grad_rows, out_weight, preferred_element_type=f32).astype(bf16)]
  transfers between devices with their start and end apart: 4 -> 4, of which waited for: 3 -> 4; matrix products, arithmetic and copies ran while one was open for 31% -> 31% of each run, Pallas kernels for 0% -> 0%
where the time goes in v1:
time: 141 us; the launch traced here: 140 us
  waiting for transfers between devices  50.6 us (36%)
  local copies, waits for them, and re-layouts  31 us (22%)
  matrix products  24.3 us (17%)
  between operations  15.7 us (11%)
  other arithmetic  10.8 us (8%)
  starting transfers between devices  8.03 us (6%)
    all_to_all x1, waiting for transfers between devices, per_device(): lax.all_to_all(presum, 'seq', split_axis=0, concat_axis=0, tiled=True)  22.4 us
    reduce_scatter x1, waiting for transfers between devices, per_device(): lax.psum_scatter(lax.dot_general(grad_rows, attn_flat, (((0,), (0,)), (()...  11.5 us
    ppermute x1, waiting for transfers between devices, grow_blocks(): other = lax.ppermute(blocks, axis, [(i, i ^ bit) for i in range(size)])  9.71 us
    select_n x4, local copies, waits for them, and re-layouts, feature_slope(): return jnp.where(inputs > 0, 1.0, jnp.exp(jnp.minimum(inputs, 0.0)))  8.25 us
    unnamed x25, local copies, waits for them, and re-layouts  7.22 us
    all_gather x1, waiting for transfers between devices, per_device(): lax.all_gather(c_grad, 'seq', axis=0, tiled=True)  6.96 us
    all_to_all x1, starting transfers between devices, per_device(): lax.all_to_all(presum, 'seq', split_axis=0, concat_axis=0, tiled=True)  4.87 us
    dot_general x1, matrix products, per_device(): lax.dot_general(grad_rows, attn_flat, (((0,), (0,)), ((), ())), preferred...  4.79 us
  transfers between devices with their start and end apart: 4, of which 4 were waited for; matrix products, arithmetic and copies ran while one was open for 31% of the time, Pallas kernels for 0%

profile of v1, /device:TPU:0, one launch (start us, length us, event | category | flops | bytes accessed | tf_op | source)
XLA Modules:
  0.0 140.4 jit_solution(64807545460536058)
XLA Ops:
  8.0 4.1 %copy.99 = bf16[1,512,2048]{1,2,0:T(8,128)(2,1)} copy(bf16[1,512,2048]{2,1,0:T(8,128)(2,1)} %param.11) | data formatting | bytes 4194304 | tf_op args[5]
  12.1 2.9 %collective-permute-start = (bf16[1,1,512,2048]{2,3,1,0:T(8,128)(2,1)}, bf16[1,1,512,2048]{2,3,1,0:T(8,128)(2,1)}, u32[]{:S(2)}, u32[]{:S(2)}) collective-permute-start(bf16[1,1,512,2048]{2,3,1,0:T(8,128)(2,1)} %bitcast.66), channel_id=1, source_target_pairs={{0,2},{2,0},{1,3},{3,1},{4,6},{6,4},{5,7},{7,5},{8,10},{10,8},{9,1... | collective-permute-start | bytes 6291464 | tf_op jit(solution)/shard_map/ppermute | solution.py:22
  19.1 4.9 %all-to-all-start = ((f32[4,2,2,128,128]{4,1,3,2,0:T(2,128)}), f32[4,2,2,128,128]{4,1,3,2,0:T(2,128)}, u32[]{:S(2)}, u32[]{:S(2)}) async-start(f32[4,2,2,128,128]{4,1,3,2,0:T(2,128)} %copy.91), calls=%async_computation | async-start | bytes 2097152 | tf_op jit(solution)/shard_map/all_to_all | solution.py:61
  27.1 22.4 %all-to-all-done = f32[4,2,2,128,128]{4,1,3,2,0:T(2,128)} async-done(((f32[4,2,2,128,128]{4,1,3,2,0:T(2,128)}), f32[4,2,2,128,128]{4,1,3,2,0:T(2,128)}, u32[]{:S(2)}, u32[]{:S(2)}) %all-to-all-start) | async-done | bytes 1048608 | tf_op jit(solution)/shard_map/all_to_all | solution.py:61
  51.3 9.7 %collective-permute-done = bf16[1,1,512,2048]{2,3,1,0:T(8,128)(2,1)} collective-permute-done((bf16[1,1,512,2048]{2,3,1,0:T(8,128)(2,1)}, bf16[1,1,512,2048]{2,3,1,0:T(8,128)(2,1)}, u32[]{:S(2)}, u32[]{:S(2)}) %collective-permute-start) | collective-permute-done | bytes 2097184 | tf_op jit(solution)/shard_map/ppermute | solution.py:22
  61.0 2.6 %pad_maximum_fusion = bf16[2,1,1,512,2048]{3,4,0,2,1:T(8,128)(2,1)S(1)} fusion(bf16[1,1,1,512,2048]{3,4,0,2,1:T(8,128)(2,1)} %bitcast.8, bf16[1,1,1,512,2048]{3,4,0,2,1:T(8,128)(2,1)} %bitcast.67), kind=kLoop, calls=%fused_computation.2 | loop fusion | flops 2097152 | bytes 8388608 | tf_op jit(solution)/shard_map/stack | solution.py:23
  64.4 1.9 %copy-done.2 = bf16[2,1,1,512,2048]{3,4,0,2,1:T(8,128)(2,1)} copy-done((bf16[2,1,1,512,2048]{3,4,0,2,1:T(8,128)(2,1)}, bf16[2,1,1,512,2048]{3,4,0,2,1:T(8,128)(2,1)S(1)}, u32[]{:S(2)}) %copy-start.2) | copy-done | bytes 4194328
  66.3 2.1 %fusion.9 = f32[512,256]{1,0:T(8,128)} fusion(bf16[512,4096]{0,1:T(8,128)(2,1)S(1)} %bitcast.68, bf16[4096,256]{1,0:T(8,128)(2,1)S(1)} %copy-done), kind=kOutput, calls=%fused_computation.20 | convolution fusion | flops 1074003968 | bytes 6815744 | tf_op jit(solution)/shard_map/dot_general | solution.py:75
  68.4 2.1 %reshape.98 = f32[2,256,2,128]{3,2,1,0:T(2,128)} reshape(f32[512,256]{1,0:T(8,128)} %fusion.9) | data formatting | bytes 1048576 | tf_op jit(solution)/shard_map/reshape | solution.py:76
  70.5 2.0 %copy.101 = f32[2,256,2,128]{1,3,2,0:T(8,128)} copy(f32[2,256,2,128]{3,2,1,0:T(2,128)} %reshape.98) | data formatting | bytes 1048576 | tf_op jit(solution)/shard_map/reshape | solution.py:76
  74.1 1.9 %subtract_convert_fusion = (bf16[2,256,2,128]{1,3,2,0:T(8,128)(2,1)S(1)}, bf16[2,256,2,128]{1,3,2,0:T(8,128)(2,1)}) fusion(f32[2,256,2,128]{1,3,2,0:T(8,128)S(1)} %get-tuple-element.15, f32[2,256,2,128]{1,3,2,0:T(8,128)} %copy.101, f32[2,256,2]{1,2,0:T(2,128)S(1)} %get-tuple-element.16, f32[2,256,2]{1,2,0:T(2,128)S(1)} %get-tuple-element.13, ...), kind=kLoop, calls=%fused_computation.40 | loop fusion | flops 917504 | bytes 1585152 | tf_op jit(solution)/shard_map/convert_element_type | solution.py:78
  77.2 1.8 %copy.98 = bf16[2,256,2,128]{3,2,1,0:T(2,128)(2,1)} copy(bf16[2,256,2,128]{1,3,2,0:T(8,128)(2,1)} %get-tuple-element.8) | data formatting | bytes 524288 | tf_op jit(solution)/shard_map/convert_element_type | solution.py:71
  79.0 4.8 %convolution_convert_fusion = bf16[4096,256]{1,0:T(8,128)(2,1)} fusion(bf16[512,4096]{0,1:T(8,128)(2,1)} %bitcast.69, bf16[64,8,2,128]{3,2,1,0:T(2,128)(2,1)} %bitcast.71), kind=kOutput, calls=%fused_computation.1 | convolution fusion | flops 1074790400 | bytes 6553600 | tf_op jit(solution)/shard_map/dot_general | solution.py:103
  83.8 2.1 %select_n.56 = f32[2,256,2,128]{3,2,1,0:T(2,128)} reshape(f32[1,512,256]{2,1,0:T(8,128)} %get-tuple-element.11) | data formatting | bytes 1048576 | tf_op jit(solution)/shard_map/jit(_where)/select_n | solution.py:34
  85.9 2.0 %copy.108 = f32[2,256,2,128]{1,3,2,0:T(8,128)} copy(f32[2,256,2,128]{3,2,1,0:T(2,128)} %select_n.56) | data formatting | bytes 1048576 | tf_op jit(solution)/shard_map/jit(_where)/select_n | solution.py:34
  88.0 2.1 %select_n.58 = f32[2,256,2,128]{3,2,1,0:T(2,128)} reshape(f32[1,512,256]{2,1,0:T(8,128)} %get-tuple-element.9) | data formatting | bytes 1048576 | tf_op jit(solution)/shard_map/jit(_where)/select_n | solution.py:34
  90.0 2.0 %copy.116 = f32[2,256,2,128]{1,3,2,0:T(8,128)} copy(f32[2,256,2,128]{3,2,1,0:T(2,128)} %select_n.58) | data formatting | bytes 1048576 | tf_op jit(solution)/shard_map/jit(_where)/select_n | solution.py:34
  92.1 1.8 %reshape_reshape.3 = bf16[1,512,256]{2,1,0:T(8,128)(2,1)} reshape(bf16[2,256,2,128]{3,2,1,0:T(2,128)(2,1)} %copy.98) | data formatting | bytes 524288 | tf_op jit(solution)/shard_map/reshape;reshape | solution.py:110
  97.3 2.0 %fusion.7 = bf16[2,256,2,128]{1,3,2,0:T(8,128)(2,1)} fusion(f32[2,256,2,128]{1,3,2,0:T(8,128)} %copy.108, f32[2,2,128,256]{3,2,1,0:T(8,128)S(1)} %fusion.42, bf16[2,256,2,128]{1,3,2,0:T(8,128)(2,1)S(1)} %get-tuple-element.7, bf16[2,2,128,128]{3,0,2,1:T(2,128)(2,1)S(1)} %reduce_sum.37), kind=kOutput, calls=%fused_computation.17 | convolution fusion | flops 33947648 | bytes 1703936 | tf_op jit(solution)/shard_map/nthe,nhde->nthd/dot_general | solution.py:90
  101.0 1.8 %reshape.93 = bf16[1,512,256]{2,1,0:T(8,128)(2,1)} reshape(bf16[2,256,2,128]{3,2,1,0:T(2,128)(2,1)} %copy.109) | data formatting | bytes 524288 | tf_op jit(solution)/shard_map/reshape | solution.py:99
  102.9 2.1 %fusion.44 = f32[2,2,128,256]{3,2,1,0:T(8,128)} fusion(bf16[2,256,2,128]{1,3,2,0:T(8,128)(2,1)S(1)} %copy.110, bf16[2,2,256,256]{3,2,1,0:T(8,128)(2,1)} %copy-done.1), kind=kOutput, calls=%fused_computation.72 | convolution fusion | flops 67108864 | bytes 1310720 | tf_op jit(solution)/shard_map/nhts,nthd->nshd/dot_general | solution.py:93
  106.0 7.0 %all-gather.2.cloned.1.call-done = f32[8,2,128,128]{3,2,1,0:T(8,128)} async-done(((f32[2,2,128,128]{3,2,1,0:T(8,128)}), f32[8,2,128,128]{3,2,1,0:T(8,128)}) %all-gather.2.cloned.1.call-update) | async-done | bytes 1048592 | tf_op jit(solution)/shard_map/all_gather | solution.py:83
  112.9 2.9 %fusion.12 = bf16[2,2,128,128]{3,0,2,1:T(2,128)(2,1)S(1)} fusion(f32[8,2,128,128]{3,2,1,0:T(8,128)} %all-gather.2.cloned.1.call-done, f32[2,8,8]{2,1,0:T(8,128)S(1)} %convert_reduce_fusion, s32[]{:T(128)S(6)} %select_n.49), kind=kOutput, calls=%fused_computation.24 | convolution fusion | flops 6356992 | bytes 1180164 | tf_op jit(solution)/shard_map/hmk,mhde->khde/dot_general | solution.py:80
  119.8 11.5 %reduce-scatter.2.cloned.1.call-done = bf16[512,256]{1,0:T(8,128)(2,1)} async-done(((bf16[4096,256]{1,0:T(8,128)(2,1)}), bf16[512,256]{1,0:T(8,128)(2,1)}) %reduce-scatter.2.cloned.1.call-update) | async-done | bytes 262160 | tf_op jit(solution)/shard_map/reduce_scatter | solution.py:102
  (58 shorter events, 24.2 us)
Async XLA Ops:
  8.0 58.3 %copy-start = (bf16[4096,256]{1,0:T(8,128)(2,1)S(1)}, bf16[4096,256]{1,0:T(8,128)(2,1)}, u32[]{:S(2)}) copy-start(bf16[4096,256]{1,0:T(8,128)(2,1)} %param.10) | copy-start | bytes 6291460
  8.0 7.0 %copy-start.9 = (bf16[1,512,256]{2,1,0:T(8,128)(2,1)S(1)}, bf16[1,512,256]{2,1,0:T(8,128)(2,1)}, u32[]{:S(2)}) copy-start(bf16[1,512,256]{2,1,0:T(8,128)(2,1)} %param.7) | copy-start | bytes 786436
  8.0 8.0 %copy-start.11 = (s32[2,8,4]{1,2,0:T(4,128)S(1)}, s32[2,8,4]{1,2,0:T(4,128)}, u32[]{:S(2)}) copy-start(s32[2,8,4]{1,2,0:T(4,128)} %param.9) | copy-start | bytes 772
  8.0 8.1 %copy-start.8 = (bf16[1,512,256]{2,1,0:T(8,128)(2,1)S(1)}, bf16[1,512,256]{2,1,0:T(8,128)(2,1)}, u32[]{:S(2)}) copy-start(bf16[1,512,256]{2,1,0:T(8,128)(2,1)} %param.8) | copy-start | bytes 786436
  12.1 48.9 %collective-permute-start = (bf16[1,1,512,2048]{2,3,1,0:T(8,128)(2,1)}, bf16[1,1,512,2048]{2,3,1,0:T(8,128)(2,1)}, u32[]{:S(2)}, u32[]{:S(2)}) collective-permute-start(bf16[1,1,512,2048]{2,3,1,0:T(8,128)(2,1)} %bitcast.66), channel_id=1, source_target_pairs={{0,2},{2,0},{1,3},{3,1},{4,6},{6,4},{5,7},{7,5},{8,10},{10,8},{9,1... | collective-permute-start | bytes 6291464 | tf_op jit(solution)/shard_map/ppermute | solution.py:22
  16.0 8.0 %copy-start.10 = (bf16[1,512,256]{2,1,0:T(8,128)(2,1)S(1)}, bf16[1,512,256]{2,1,0:T(8,128)(2,1)}, u32[]{:S(2)}) copy-start(bf16[1,512,256]{2,1,0:T(8,128)(2,1)} %param.6) | copy-start | bytes 786436
  16.2 9.1 %copy-start.3 = (bf16[2,256,2,128]{3,2,1,0:T(2,128)(2,1)}, bf16[2,256,2,128]{3,2,1,0:T(2,128)(2,1)S(1)}, u32[]{:S(2)}) copy-start(bf16[2,256,2,128]{3,2,1,0:T(2,128)(2,1)S(1)} %select_n.48) | copy-start | bytes 786436
  16.4 8.6 %copy-start.5 = (bf16[2,256,2,128]{1,3,2,0:T(8,128)(2,1)}, bf16[2,256,2,128]{1,3,2,0:T(8,128)(2,1)S(1)}, u32[]{:S(2)}) copy-start(bf16[2,256,2,128]{1,3,2,0:T(8,128)(2,1)S(1)} %copy.87) | copy-start | bytes 786436
  19.1 30.4 %all-to-all-start = ((f32[4,2,2,128,128]{4,1,3,2,0:T(2,128)}), f32[4,2,2,128,128]{4,1,3,2,0:T(2,128)}, u32[]{:S(2)}, u32[]{:S(2)}) async-start(f32[4,2,2,128,128]{4,1,3,2,0:T(2,128)} %copy.91), calls=%async_computation | async-start | bytes 2097152 | tf_op jit(solution)/shard_map/all_to_all | solution.py:61
  24.0 88.9 %all-gather.2.cloned.1.call-start = ((), (), s32[]{:S(2)}) async-start(), calls=%async_computation.2 | async-start | bytes 1310720 | tf_op jit(solution)/shard_map/all_gather | solution.py:83
  25.3 0.7 copy-start.6
  64.4 2.0 %copy-start.2 = (bf16[2,1,1,512,2048]{3,4,0,2,1:T(8,128)(2,1)}, bf16[2,1,1,512,2048]{3,4,0,2,1:T(8,128)(2,1)S(1)}, u32[]{:S(2)}) copy-start(bf16[2,1,1,512,2048]{3,4,0,2,1:T(8,128)(2,1)S(1)} %reverse_select_fusion) | copy-start | bytes 12582916
  77.0 54.3 %reduce-scatter.2.cloned.1.call-start = ((), (), s32[]{:S(2)}) async-start(), calls=%async_computation.3 | async-start | bytes 2359296 | tf_op jit(solution)/shard_map/reduce_scatter | solution.py:102
  95.2 0.8 copy-start.1
  104.9 13.6 %copy-start.4 = (bf16[2,256,2,128]{3,2,1,0:T(2,128)(2,1)S(1)}, bf16[2,256,2,128]{3,2,1,0:T(2,128)(2,1)}, u32[]{:S(2)}) copy-start(bf16[2,256,2,128]{3,2,1,0:T(2,128)(2,1)} %copy-done.3) | copy-start | bytes 786436
  106.0 12.5 %copy-start.7 = (f32[2,2,128,256]{3,2,1,0:T(8,128)S(1)}, f32[2,2,128,256]{3,2,1,0:T(8,128)}, u32[]{:S(2)}) copy-start(f32[2,2,128,256]{3,2,1,0:T(8,128)} %fusion.45) | copy-start | bytes 1572868
Sparse Core Ops, SparseCore 0:
  77.1 35.7 all-gather.1
Sparse Core Ops, SparseCore 1:
  83.9 47.3 reduce-scatter.1
